TPU v7x, 32 devices: a whole 2x2x4 slice. The times are simulated.
32 devices in a mesh: blk: 8 (over y, x, core), rows: 4 (over z).
Axes of the slice: x: 2, y: 2, z: 4, core: 2. Of those that a mesh axis runs over, the one named last changes fastest.
Arguments:
- sens_tiles: bfloat16 [2048, 512, 128], P('blk', 'rows'), may hold values from -1 to 1
- start_basis: bfloat16 [64, 32768], P(None, 'blk'), may hold values from -6 to 6
- row_blocks: int32 [2048, 4], P('blk', 'rows'), may hold values from 0 to 7, as said below
- col_blocks: int32 [2048, 4], P('blk', 'rows'), may hold values from 0 to 31, as said below
- live_counts: int32 [8, 4], P('blk', 'rows'), may hold values from 64 to 256, as said below
Outputs:
- orthonormal: float32 [4, 64, 32768], P(None, None, ('blk', 'rows'))
Inputs may be any that keep to these rules, and one draw needn't show every extreme that they name: Within one device the pairs (row_blocks, col_blocks) of its 256 slots are distinct. Within one device the pairs (row_blocks, col_blocks) of its 256 slots are distinct. Slots 0 to live_counts - 1 of a device hold its tiles; some device has all 256 slots live.
All inputs are finite; a program needn't handle non-finite values.
Results may differ from a plain program's by a relative error of at most 0.012.
The roundings to bfloat16 on the way count: a program that leaves them out, or rounds other values in their place, can miss the bound.
Values may be sent and summed in bfloat16 or wider, within the bound.
A program may use at most 128 MiB of HBM per device.

v0:
```python
import jax
import jax.numpy as jnp
from jax import lax
from jax.sharding import PartitionSpec as P

RB = 8
CB = 32
ITERS = 4


def apply_forward(sens_tiles, basis_now, col_slots, row_onehot):
    vectors = basis_now.shape[0]
    tile_size = sens_tiles.shape[2]
    picked = jnp.take(basis_now.reshape(vectors, CB, tile_size), col_slots, axis=1)
    products = jnp.einsum("kst,sit->ksi", picked, sens_tiles, preferred_element_type=jnp.float32)
    summed = jnp.einsum("ksi,rs->kri", products, row_onehot, precision=lax.Precision.HIGHEST)
    return summed.reshape(vectors, RB * tile_size)


def apply_backward(sens_tiles, image_half, row_slots, col_onehot):
    vectors = image_half.shape[0]
    tile_size = sens_tiles.shape[2]
    picked = jnp.take(image_half.reshape(vectors, RB, tile_size), row_slots, axis=1)
    products = jnp.einsum("ksi,sij->ksj", picked, sens_tiles, preferred_element_type=jnp.float32)
    summed = jnp.einsum("ksj,cs->kcj", products, col_onehot, precision=lax.Precision.HIGHEST)
    return summed.reshape(vectors, CB * tile_size)


def factor_whole(current, total):
    local_gram = jnp.dot(current, current.T, precision=lax.Precision.HIGHEST)
    gram = lax.psum(local_gram, "blk") / total
    lower = jnp.linalg.cholesky(gram)
    return jax.scipy.linalg.solve_triangular(lower, current, lower=True)


def local(sens_tiles, start_basis, row_blocks, col_blocks, live_counts):
    row_slots = row_blocks[:, 0]
    col_slots = col_blocks[:, 0]
    count_live = live_counts[0, 0]
    slot_total = sens_tiles.shape[0]
    tile_size = sens_tiles.shape[2]
    live = jnp.arange(slot_total) < count_live
    row_onehot = ((row_slots[None, :] == jnp.arange(RB)[:, None]) & live[None, :]).astype(
        jnp.float32
    )
    col_onehot = ((col_slots[None, :] == jnp.arange(CB)[:, None]) & live[None, :]).astype(
        jnp.float32
    )
    total = float(CB * tile_size * lax.axis_size("blk"))
    own_width = CB * tile_size // lax.axis_size("rows")
    basis_now = start_basis
    results = []
    for iteration in range(ITERS):
        partial_image = apply_forward(sens_tiles, basis_now, col_slots, row_onehot)
        image = lax.psum(partial_image, "blk")
        image_half = image.astype(jnp.bfloat16)
        partial_hessian = apply_backward(sens_tiles, image_half, row_slots, col_onehot)
        hessian = lax.psum(partial_hessian, "rows")
        whole_result = factor_whole(hessian, total)
        basis_now = whole_result.astype(jnp.bfloat16)
        result = lax.dynamic_slice_in_dim(
            whole_result, lax.axis_index("rows") * own_width, own_width, 1
        )
        results.append(result)
    return jnp.stack(results, axis=0)


def solution(mesh):
    in_specs = (
        P("blk", "rows", None),
        P(None, "blk"),
        P("blk", "rows"),
        P("blk", "rows"),
        P("blk", "rows"),
    )
    out_specs = P(None, None, ("blk", "rows"))
    return jax.shard_map(local, mesh=mesh, in_specs=in_specs, out_specs=out_specs, check_vma=False)
```

profile of v0, /device:TPU:0, one launch (start us, length us, event | category | flops | bytes accessed | tf_op | source)
XLA Modules:
  0.0 653.3 jit_solution(9419659961309902612)
XLA Ops:
  12.5 10.4 %fusion.48 = f32[64,256,128]{2,0,1:T(8,128)S(1)} fusion(bf16[256,128,128]{2,1,0:T(8,128)(2,1)} %param.12, bf16[256,64,128]{2,1,0:T(8,128)(2,1)} %gather_fusion, pred[256]{0:T(512)(128)(4,1)S(1)} %get-tuple-element.8), kind=kOutput, calls=%fused_computation.56 | convolution fusion | flops 538968064 | bytes 20971776 | tf_op jit(solution)/shard_map/kst,sit->ksi/dot_general | solution.py:15
  22.9 7.5 %fusion.14 = f32[8,64,128]{2,0,1:T(8,128)S(1)} fusion(f32[64,256,128]{2,0,1:T(8,128)S(1)} %fusion.48, s32[256]{0:T(256)S(1)} %bitcast.242, pred[256]{0:T(512)(128)(4,1)S(1)} %iota_compare_fusion.4), kind=kOutput, calls=%fused_computation.22 | convolution fusion | flops 201330688 | bytes 8652032 | tf_op jit(solution)/shard_map/ksi,rs->kri/dot_general | solution.py:16
  30.8 28.4 %all-reduce.16 = bf16[64,1024]{1,0:T(8,128)(2,1)S(1)} all-reduce(f32[64,1024]{1,0:T(8,128)S(1)} %bitcast.236), channel_id=1, replica_groups=mesh['blk'=8,'rows'=4] {'blk'}, use_global_device_ids=true, to_apply=%region_0.0 | all-reduce | flops 65536 | bytes 393216 | tf_op jit(solution)/shard_map/psum | solution.py:55
  62.3 7.0 %fusion.51 = f32[64,256,128]{2,0,1:T(8,128)S(1)} fusion(bf16[256,128,128]{2,1,0:T(8,128)(2,1)} %param.12, bf16[256,64,128]{2,1,0:T(8,128)(2,1)} %gather_fusion.1, pred[256]{0:T(512)(128)(4,1)S(1)} %get-tuple-element.6), kind=kOutput, calls=%fused_computation.57 | convolution fusion | flops 538968064 | bytes 20971776 | tf_op jit(solution)/shard_map/ksi,sij->ksj/dot_general | solution.py:24
  69.4 7.7 %fusion.12 = f32[32,64,128]{2,0,1:T(8,128)S(1)} fusion(f32[64,256,128]{2,0,1:T(8,128)S(1)} %fusion.51, s32[256]{0:T(256)S(1)} %bitcast.248, pred[256]{0:T(512)(128)(4,1)S(1)} %iota_compare_fusion.4), kind=kOutput, calls=%fused_computation.20 | convolution fusion | flops 805322752 | bytes 9438464 | tf_op jit(solution)/shard_map/ksj,cs->kcj/dot_general | solution.py:25
  78.7 51.6 %all-reduce.9.cloned.1.call-done = f32[64,4096]{1,0:T(8,128)} async-done(((f32[64,4096]{1,0:T(8,128)}), f32[64,4096]{1,0:T(8,128)}) %all-reduce.9.cloned.1.call-update) | async-done | bytes 1048592 | tf_op jit(solution)/shard_map/psum | solution.py:58
  132.8 24.3 %psum.86 = f32[64,64]{0,1:T(8,128)S(1)} all-reduce(f32[64,64]{0,1:T(8,128)S(1)} %fusion.116), channel_id=1, replica_groups=mesh['blk'=8,'rows'=4] {'blk'}, use_global_device_ids=true, to_apply=%region_2.0 | all-reduce | flops 4096 | bytes 32768 | tf_op jit(solution)/shard_map/psum | solution.py:31
  157.2 5.8 cholesky.74
  175.7 10.4 %fusion.54 = f32[64,256,128]{2,0,1:T(8,128)S(1)} fusion(bf16[256,128,128]{2,1,0:T(8,128)(2,1)} %param.12, bf16[256,64,128]{2,1,0:T(8,128)(2,1)} %gather_fusion.2, pred[256]{0:T(512)(128)(4,1)S(1)} %get-tuple-element.8), kind=kOutput, calls=%fused_computation.58 | convolution fusion | flops 538968064 | bytes 20971776 | tf_op jit(solution)/shard_map/kst,sit->ksi/dot_general | solution.py:15
  186.1 7.9 %fusion.10 = f32[8,64,128]{2,0,1:T(8,128)S(1)} fusion(f32[64,256,128]{2,0,1:T(8,128)S(1)} %fusion.54, s32[256]{0:T(256)S(1)} %bitcast.243, pred[256]{0:T(512)(128)(4,1)S(1)} %iota_compare_fusion.4), kind=kOutput, calls=%fused_computation.18 | convolution fusion | flops 201330688 | bytes 8652032 | tf_op jit(solution)/shard_map/ksi,rs->kri/dot_general | solution.py:16
  194.0 25.3 %all-reduce.17 = bf16[64,1024]{1,0:T(8,128)(2,1)S(1)} all-reduce(f32[64,1024]{1,0:T(8,128)S(1)} %bitcast.237), channel_id=1, replica_groups=mesh['blk'=8,'rows'=4] {'blk'}, use_global_device_ids=true, to_apply=%region_5.10 | all-reduce | flops 65536 | bytes 393216 | tf_op jit(solution)/shard_map/psum | solution.py:55
  222.3 7.0 %fusion.57 = f32[64,256,128]{2,0,1:T(8,128)S(1)} fusion(bf16[256,128,128]{2,1,0:T(8,128)(2,1)} %param.12, bf16[256,64,128]{2,1,0:T(8,128)(2,1)} %gather_fusion.3, pred[256]{0:T(512)(128)(4,1)S(1)} %get-tuple-element.6), kind=kOutput, calls=%fused_computation.59 | convolution fusion | flops 538968064 | bytes 20971776 | tf_op jit(solution)/shard_map/ksi,sij->ksj/dot_general | solution.py:24
  229.4 7.7 %fusion.8 = f32[32,64,128]{2,0,1:T(8,128)S(1)} fusion(f32[64,256,128]{2,0,1:T(8,128)S(1)} %fusion.57, s32[256]{0:T(256)S(1)} %bitcast.249, pred[256]{0:T(512)(128)(4,1)S(1)} %iota_compare_fusion.4), kind=kOutput, calls=%fused_computation.16 | convolution fusion | flops 805322752 | bytes 9438464 | tf_op jit(solution)/shard_map/ksj,cs->kcj/dot_general | solution.py:25
  238.8 49.5 %all-reduce.11.cloned.1.call-done = f32[64,4096]{1,0:T(8,128)} async-done(((f32[64,4096]{1,0:T(8,128)}), f32[64,4096]{1,0:T(8,128)}) %all-reduce.11.cloned.1.call-update) | async-done | bytes 1048592 | tf_op jit(solution)/shard_map/psum | solution.py:58
  290.7 24.3 %psum.89 = f32[64,64]{0,1:T(8,128)S(1)} all-reduce(f32[64,64]{0,1:T(8,128)S(1)} %fusion.117), channel_id=1, replica_groups=mesh['blk'=8,'rows'=4] {'blk'}, use_global_device_ids=true, to_apply=%region_7.12 | all-reduce | flops 4096 | bytes 32768 | tf_op jit(solution)/shard_map/psum | solution.py:31
  315.1 5.8 cholesky.85
  333.6 10.4 %fusion.60 = f32[64,256,128]{2,0,1:T(8,128)S(1)} fusion(bf16[256,128,128]{2,1,0:T(8,128)(2,1)} %param.12, bf16[256,64,128]{2,1,0:T(8,128)(2,1)} %gather_fusion.4, pred[256]{0:T(512)(128)(4,1)S(1)} %get-tuple-element.8), kind=kOutput, calls=%fused_computation.60 | convolution fusion | flops 538968064 | bytes 20971776 | tf_op jit(solution)/shard_map/kst,sit->ksi/dot_general | solution.py:15
  344.0 7.9 %fusion.6 = f32[8,64,128]{2,0,1:T(8,128)S(1)} fusion(f32[64,256,128]{2,0,1:T(8,128)S(1)} %fusion.60, s32[256]{0:T(256)S(1)} %bitcast.244, pred[256]{0:T(512)(128)(4,1)S(1)} %iota_compare_fusion.4), kind=kOutput, calls=%fused_computation.14 | convolution fusion | flops 201330688 | bytes 8652032 | tf_op jit(solution)/shard_map/ksi,rs->kri/dot_general | solution.py:16
  352.0 25.3 %all-reduce.18 = bf16[64,1024]{1,0:T(8,128)(2,1)S(1)} all-reduce(f32[64,1024]{1,0:T(8,128)S(1)} %bitcast.238), channel_id=1, replica_groups=mesh['blk'=8,'rows'=4] {'blk'}, use_global_device_ids=true, to_apply=%region_8.13 | all-reduce | flops 65536 | bytes 393216 | tf_op jit(solution)/shard_map/psum | solution.py:55
  380.3 7.0 %fusion.63 = f32[64,256,128]{2,0,1:T(8,128)S(1)} fusion(bf16[256,128,128]{2,1,0:T(8,128)(2,1)} %param.12, bf16[256,64,128]{2,1,0:T(8,128)(2,1)} %gather_fusion.5, pred[256]{0:T(512)(128)(4,1)S(1)} %get-tuple-element.6), kind=kOutput, calls=%fused_computation.61 | convolution fusion | flops 538968064 | bytes 20971776 | tf_op jit(solution)/shard_map/ksi,sij->ksj/dot_general | solution.py:24
  387.3 7.7 %fusion.4 = f32[32,64,128]{2,0,1:T(8,128)S(1)} fusion(f32[64,256,128]{2,0,1:T(8,128)S(1)} %fusion.63, s32[256]{0:T(256)S(1)} %bitcast.250, pred[256]{0:T(512)(128)(4,1)S(1)} %iota_compare_fusion.4), kind=kOutput, calls=%fused_computation.12 | convolution fusion | flops 805322752 | bytes 9438464 | tf_op jit(solution)/shard_map/ksj,cs->kcj/dot_general | solution.py:25
  396.7 49.5 %all-reduce.13.cloned.1.call-done = f32[64,4096]{1,0:T(8,128)} async-done(((f32[64,4096]{1,0:T(8,128)}), f32[64,4096]{1,0:T(8,128)}) %all-reduce.13.cloned.1.call-update) | async-done | bytes 1048592 | tf_op jit(solution)/shard_map/psum | solution.py:58
  448.7 24.2 %psum.92 = f32[64,64]{0,1:T(8,128)S(1)} all-reduce(f32[64,64]{0,1:T(8,128)S(1)} %fusion.118), channel_id=1, replica_groups=mesh['blk'=8,'rows'=4] {'blk'}, use_global_device_ids=true, to_apply=%region_10.15 | all-reduce | flops 4096 | bytes 32768 | tf_op jit(solution)/shard_map/psum | solution.py:31
  473.1 5.8 cholesky.96
  491.6 10.4 %fusion.66 = f32[64,256,128]{2,0,1:T(8,128)S(1)} fusion(bf16[256,128,128]{2,1,0:T(8,128)(2,1)} %param.12, bf16[256,64,128]{2,1,0:T(8,128)(2,1)} %gather_fusion.6, pred[256]{0:T(512)(128)(4,1)S(1)} %get-tuple-element.8), kind=kOutput, calls=%fused_computation.62 | convolution fusion | flops 538968064 | bytes 20971776 | tf_op jit(solution)/shard_map/kst,sit->ksi/dot_general | solution.py:15
  501.9 7.7 %fusion.2 = f32[8,64,128]{2,0,1:T(8,128)S(1)} fusion(f32[64,256,128]{2,0,1:T(8,128)S(1)} %fusion.66, s32[256]{0:T(256)S(1)} %bitcast.245, pred[256]{0:T(512)(128)(4,1)S(1)} %iota_compare_fusion.4), kind=kOutput, calls=%fused_computation.10 | convolution fusion | flops 201330688 | bytes 8652032 | tf_op jit(solution)/shard_map/ksi,rs->kri/dot_general | solution.py:16
  509.7 25.3 %all-reduce.19 = bf16[64,1024]{1,0:T(8,128)(2,1)S(1)} all-reduce(f32[64,1024]{1,0:T(8,128)S(1)} %bitcast.239), channel_id=1, replica_groups=mesh['blk'=8,'rows'=4] {'blk'}, use_global_device_ids=true, to_apply=%region_11.16 | all-reduce | flops 65536 | bytes 393216 | tf_op jit(solution)/shard_map/psum | solution.py:55
  538.0 7.0 %fusion.69 = f32[64,256,128]{2,0,1:T(8,128)S(1)} fusion(bf16[256,128,128]{2,1,0:T(8,128)(2,1)} %param.12, bf16[256,64,128]{2,1,0:T(8,128)(2,1)} %gather_fusion.7, pred[256]{0:T(512)(128)(4,1)S(1)} %get-tuple-element.6), kind=kOutput, calls=%fused_computation.63 | convolution fusion | flops 538968064 | bytes 20971776 | tf_op jit(solution)/shard_map/ksi,sij->ksj/dot_general | solution.py:24
  545.1 7.7 %fusion = f32[32,64,128]{2,0,1:T(8,128)S(1)} fusion(f32[64,256,128]{2,0,1:T(8,128)S(1)} %fusion.69, s32[256]{0:T(256)S(1)} %bitcast.251, pred[256]{0:T(512)(128)(4,1)S(1)} %iota_compare_fusion.4), kind=kOutput, calls=%fused_computation.8 | convolution fusion | flops 805322752 | bytes 9438464 | tf_op jit(solution)/shard_map/ksj,cs->kcj/dot_general | solution.py:25
  557.4 46.5 %all-reduce.15.cloned.1.call-done = f32[64,4096]{1,0:T(8,128)} async-done(((f32[64,4096]{1,0:T(8,128)}), f32[64,4096]{1,0:T(8,128)}) %all-reduce.15.cloned.1.call-update) | async-done | bytes 1048592 | tf_op jit(solution)/shard_map/psum | solution.py:58
  606.7 24.1 %psum.95 = f32[64,64]{0,1:T(8,128)S(1)} all-reduce(f32[64,64]{0,1:T(8,128)S(1)} %fusion.119), channel_id=1, replica_groups=mesh['blk'=8,'rows'=4] {'blk'}, use_global_device_ids=true, to_apply=%region_13.18 | all-reduce | flops 4096 | bytes 32768 | tf_op jit(solution)/shard_map/psum | solution.py:31
  630.9 5.8 cholesky.107
  (93 shorter events, 85.7 us)
Async XLA Ops:
  6.5 2.8 copy-start
  6.5 123.8 %all-reduce.9.cloned.1.call-start = ((), (), s32[]{:S(2)}) async-start(), calls=%async_computation | async-start | bytes 2097152 | tf_op jit(solution)/shard_map/psum | solution.py:58
  12.5 10.4 %copy-start.5 = (s32[256,1]{0,1:T(1,128)S(1)}, s32[256,1]{0,1:T(1,128)}, u32[]{:S(2)}) copy-start(s32[256,1]{0,1:T(1,128)} %param.14) | copy-start | bytes 3076
  62.3 7.0 %copy-start.6 = (s32[256,1]{0,1:T(1,128)S(1)}, s32[256,1]{0,1:T(1,128)}, u32[]{:S(2)}) copy-start(s32[256,1]{0,1:T(1,128)} %param.15) | copy-start | bytes 3076
  78.7 209.5 %all-reduce.11.cloned.1.call-start = ((), (), s32[]{:S(2)}) async-start(), calls=%async_computation.1 | async-start | bytes 2097152 | tf_op jit(solution)/shard_map/psum | solution.py:58
  171.6 1.0 copy-start.2
  238.7 207.5 %all-reduce.13.cloned.1.call-start = ((), (), s32[]{:S(2)}) async-start(), calls=%async_computation.2 | async-start | bytes 2097152 | tf_op jit(solution)/shard_map/psum | solution.py:58
  329.5 1.0 copy-start.3
  396.7 207.2 %all-reduce.15.cloned.1.call-start = ((), (), s32[]{:S(2)}) async-start(), calls=%async_computation.3 | async-start | bytes 2097152 | tf_op jit(solution)/shard_map/psum | solution.py:58
  487.4 1.0 copy-start.4
  554.4 91.9 %copy-start.1 = (bf16[64,4096]{1,0:T(8,128)(2,1)S(1)}, bf16[64,4096]{1,0:T(8,128)(2,1)}, u32[]{:S(2)}) copy-start(bf16[64,4096]{1,0:T(8,128)(2,1)} %param.13) | copy-start | bytes 1572868
Sparse Core Ops, SparseCore 0:
  78.8 51.4 all-reduce.8
  238.8 49.3 all-reduce.10
  396.8 49.3 all-reduce.12
  554.5 49.3 all-reduce.14
where the time goes:
time: 663 us; the launch traced here: 653 us
  blocking collectives  201 us (30%)
  waiting for transfers between devices  197 us (30%)
  matrix products  151 us (23%)
  other arithmetic  51.9 us (8%)
  local copies, waits for them, and re-layouts  37.5 us (6%)
  between operations  14.7 us (2%)
    psum x4, waiting for transfers between devices, local(): hessian = lax.psum(partial_hessian, 'rows')  197 us
    psum x4, blocking collectives, local(): image = lax.psum(partial_image, 'blk')  104 us
    psum x4, blocking collectives, factor_whole(): gram = lax.psum(local_gram, 'blk') / total  96.9 us
    dot_general x4, matrix products, apply_forward(): jnp.einsum('kst,sit->ksi', picked, sens_tiles, preferred_element_type=jnp...  41.5 us
    dot_general x4, matrix products, apply_forward(): jnp.einsum('ksi,rs->kri', products, row_onehot, precision=lax.Precision.H...  31 us
    dot_general x4, matrix products, apply_backward(): jnp.einsum('ksj,cs->kcj', products, col_onehot, precision=lax.Precision.H...  30.9 us
    dot_general x4, matrix products, apply_backward(): jnp.einsum('ksi,sij->ksj', picked, sens_tiles, preferred_element_type=jnp...  28.1 us
    another operation x12, other arithmetic, factor_whole(): lower = jnp.linalg.cholesky(gram)  26.1 us
  transfers between devices with their start and end apart: 4, of which 4 were waited for; matrix products, arithmetic and copies ran while one was open for 0% of the time, Pallas kernels for 0%

commit v1 on v0

--- a/solution.py
+++ b/solution.py
@@ -55,7 +55,11 @@
         image = lax.psum(partial_image, "blk")
         image_half = image.astype(jnp.bfloat16)
         partial_hessian = apply_backward(sens_tiles, image_half, row_slots, col_onehot)
-        hessian = lax.psum(partial_hessian, "rows")
+        hessian = partial_hessian
+        for hop in (1, 2):
+            hessian = hessian + lax.ppermute(
+                hessian, "rows", [(dev, dev ^ hop) for dev in range(4)]
+            )
         whole_result = factor_whole(hessian, total)
         basis_now = whole_result.astype(jnp.bfloat16)
         result = lax.dynamic_slice_in_dim(

time: 663 us -> 733 us (1.11)
  waiting for transfers between devices: 197 us -> 252 us
  starting transfers between devices: 0.13 us -> 18.2 us
  other arithmetic: 51.9 us -> 66.6 us
  between operations: 14.7 us -> 1.61 us
  blocking collectives: 201 us -> 213 us
  matrix products: 151 us -> 140 us
    ppermute x0 -> x8, waiting for transfers between devices: none -> 252 us  [local(): lax.ppermute(hessian, 'rows', [(dev, dev ^ hop) for dev in range(4)])]
    psum x4 -> x0, waiting for transfers between devices: 197 us -> none  [local(): hessian = lax.psum(partial_hessian, 'rows')]
    ppermute x0 -> x8, starting transfers between devices: none -> 18.2 us  [local(): lax.ppermute(hessian, 'rows', [(dev, dev ^ hop) for dev in range(4)])]
    add x0 -> x8, other arithmetic: none -> 14.7 us  [local(): hessian + lax.ppermute(hessian, 'rows', [(dev, dev ^ hop) for dev in rang...]
    psum x4, blocking collectives: 96.9 us -> 108 us  [factor_whole(): gram = lax.psum(local_gram, 'blk') / total]
  transfers between devices with their start and end apart: 4 -> 8, of which waited for: 4 -> 8; matrix products, arithmetic and copies ran while one was open for 0% -> 0% of each run, Pallas kernels for 0% -> 0%
where the time goes in v1:
time: 733 us; the launch traced here: 724 us
  waiting for transfers between devices  252 us (34%)
  blocking collectives  213 us (29%)
  matrix products  140 us (19%)
  other arithmetic  66.6 us (9%)
  local copies, waits for them, and re-layouts  33.5 us (5%)
  starting transfers between devices  18.2 us (2%)
    ppermute x8, waiting for transfers between devices, local(): lax.ppermute(hessian, 'rows', [(dev, dev ^ hop) for dev in range(4)])  252 us
    psum x4, blocking collectives, factor_whole(): gram = lax.psum(local_gram, 'blk') / total  108 us
    psum x4, blocking collectives, local(): image = lax.psum(partial_image, 'blk')  104 us
    dot_general x4, matrix products, apply_forward(): jnp.einsum('kst,sit->ksi', picked, sens_tiles, preferred_element_type=jnp...  41.5 us
    dot_general x4, matrix products, apply_forward(): jnp.einsum('ksi,rs->kri', products, row_onehot, precision=lax.Precision.H...  31 us
    dot_general x4, matrix products, apply_backward(): jnp.einsum('ksj,cs->kcj', products, col_onehot, precision=lax.Precision.H...  30.9 us
    dot_general x4, matrix products, apply_backward(): jnp.einsum('ksi,sij->ksj', picked, sens_tiles, preferred_element_type=jnp...  28.1 us
    another operation x12, other arithmetic, factor_whole(): lower = jnp.linalg.cholesky(gram)  26.1 us
  transfers between devices with their start and end apart: 8, of which 8 were waited for; matrix products, arithmetic and copies ran while one was open for 0% of the time, Pallas kernels for 0%

profile of v1, /device:TPU:0, one launch (start us, length us, event | category | flops | bytes accessed | tf_op | source)
XLA Modules:
  0.0 724.2 jit_solution(9180322870415601021)
XLA Ops:
  6.0 10.4 %fusion.48 = f32[64,256,128]{2,0,1:T(8,128)S(1)} fusion(bf16[256,128,128]{2,1,0:T(8,128)(2,1)} %param.12, bf16[256,64,128]{2,1,0:T(8,128)(2,1)} %gather_fusion, pred[256]{0:T(512)(128)(4,1)S(1)} %get-tuple-element.8), kind=kOutput, calls=%fused_computation.56 | convolution fusion | flops 538968064 | bytes 20971776 | tf_op jit(solution)/shard_map/kst,sit->ksi/dot_general | solution.py:15
  16.4 7.5 %fusion.14 = f32[8,64,128]{2,0,1:T(8,128)S(1)} fusion(f32[64,256,128]{2,0,1:T(8,128)S(1)} %fusion.48, s32[256]{0:T(256)S(1)} %bitcast.254, pred[256]{0:T(512)(128)(4,1)S(1)} %iota_compare_fusion.4), kind=kOutput, calls=%fused_computation.22 | convolution fusion | flops 201330688 | bytes 8652032 | tf_op jit(solution)/shard_map/ksi,rs->kri/dot_general | solution.py:16
  24.2 28.4 %all-reduce.4 = bf16[64,1024]{1,0:T(8,128)(2,1)S(1)} all-reduce(f32[64,1024]{1,0:T(8,128)S(1)} %bitcast.248), channel_id=1, replica_groups=mesh['blk'=8,'rows'=4] {'blk'}, use_global_device_ids=true, to_apply=%region_0.0 | all-reduce | flops 65536 | bytes 393216 | tf_op jit(solution)/shard_map/psum | solution.py:55
  55.7 7.0 fusion.51
  62.7 7.7 %fusion.12 = f32[32,64,128]{2,0,1:T(8,128)S(1)} fusion(f32[64,256,128]{2,0,1:T(8,128)S(1)} %fusion.51, s32[256]{0:T(256)S(1)} %bitcast.260, pred[256]{0:T(512)(128)(4,1)S(1)} %iota_compare_fusion.4), kind=kOutput, calls=%fused_computation.20 | convolution fusion | flops 805322752 | bytes 9438464 | tf_op jit(solution)/shard_map/ksj,cs->kcj/dot_general | solution.py:25
  72.7 20.8 %collective-permute-done = f32[64,4096]{1,0:T(8,128)S(1)} collective-permute-done((f32[64,4096]{1,0:T(8,128)S(1)}, f32[64,4096]{1,0:T(8,128)S(1)}, u32[]{:S(2)}, u32[]{:S(2)}) %collective-permute-start) | collective-permute-done | bytes 1048608 | tf_op jit(solution)/shard_map/ppermute | solution.py:60
  93.5 10.4 %fusion.116 = f32[64,4096]{1,0:T(8,128)S(1)} fusion(f32[64,4096]{1,0:T(8,128)S(1)} %collective-permute-done, f32[8,8,32,128]{3,2,1,0:T(8,128)S(1)} %bitcast.235), kind=kLoop, calls=%fused_computation.159 | loop fusion | flops 262144 | bytes 3145728 | tf_op jit(solution)/shard_map/add | solution.py:60
  106.5 42.2 %collective-permute-done.1 = f32[64,4096]{1,0:T(8,128)S(1)} collective-permute-done((f32[64,4096]{1,0:T(8,128)S(1)}, f32[64,4096]{1,0:T(8,128)S(1)}, u32[]{:S(2)}, u32[]{:S(2)}) %collective-permute-start.1) | collective-permute-done | bytes 1048608 | tf_op jit(solution)/shard_map/ppermute | solution.py:60
  149.9 27.9 %psum.57 = f32[64,64]{0,1:T(8,128)S(1)} all-reduce(f32[64,64]{0,1:T(8,128)S(1)} %fusion.120), channel_id=1, replica_groups=mesh['blk'=8,'rows'=4] {'blk'}, use_global_device_ids=true, to_apply=%region_1.0 | all-reduce | flops 4096 | bytes 32768 | tf_op jit(solution)/shard_map/psum | solution.py:31
  195.1 10.4 %fusion.54 = f32[64,256,128]{2,0,1:T(8,128)S(1)} fusion(bf16[256,128,128]{2,1,0:T(8,128)(2,1)} %param.12, bf16[256,64,128]{2,1,0:T(8,128)(2,1)} %gather_fusion.2, pred[256]{0:T(512)(128)(4,1)S(1)} %get-tuple-element.8), kind=kOutput, calls=%fused_computation.58 | convolution fusion | flops 538968064 | bytes 20971776 | tf_op jit(solution)/shard_map/kst,sit->ksi/dot_general | solution.py:15
  205.5 7.9 %fusion.10 = f32[8,64,128]{2,0,1:T(8,128)S(1)} fusion(f32[64,256,128]{2,0,1:T(8,128)S(1)} %fusion.54, s32[256]{0:T(256)S(1)} %bitcast.255, pred[256]{0:T(512)(128)(4,1)S(1)} %iota_compare_fusion.4), kind=kOutput, calls=%fused_computation.18 | convolution fusion | flops 201330688 | bytes 8652032 | tf_op jit(solution)/shard_map/ksi,rs->kri/dot_general | solution.py:16
  213.4 25.5 %all-reduce.5 = bf16[64,1024]{1,0:T(8,128)(2,1)S(1)} all-reduce(f32[64,1024]{1,0:T(8,128)S(1)} %bitcast.249), channel_id=1, replica_groups=mesh['blk'=8,'rows'=4] {'blk'}, use_global_device_ids=true, to_apply=%region_4.9 | all-reduce | flops 65536 | bytes 393216 | tf_op jit(solution)/shard_map/psum | solution.py:55
  241.9 7.0 fusion.57
  249.0 7.7 %fusion.8 = f32[32,64,128]{2,0,1:T(8,128)S(1)} fusion(f32[64,256,128]{2,0,1:T(8,128)S(1)} %fusion.57, s32[256]{0:T(256)S(1)} %bitcast.261, pred[256]{0:T(512)(128)(4,1)S(1)} %iota_compare_fusion.4), kind=kOutput, calls=%fused_computation.16 | convolution fusion | flops 805322752 | bytes 9438464 | tf_op jit(solution)/shard_map/ksj,cs->kcj/dot_general | solution.py:25
  258.9 20.9 %collective-permute-done.2 = f32[64,4096]{1,0:T(8,128)S(1)} collective-permute-done((f32[64,4096]{1,0:T(8,128)S(1)}, f32[64,4096]{1,0:T(8,128)S(1)}, u32[]{:S(2)}, u32[]{:S(2)}) %collective-permute-start.2) | collective-permute-done | bytes 1048608 | tf_op jit(solution)/shard_map/ppermute | solution.py:60
  283.9 42.6 %collective-permute-done.3 = f32[64,4096]{1,0:T(8,128)S(1)} collective-permute-done((f32[64,4096]{1,0:T(8,128)S(1)}, f32[64,4096]{1,0:T(8,128)S(1)}, u32[]{:S(2)}, u32[]{:S(2)}) %collective-permute-start.3) | collective-permute-done | bytes 1048608 | tf_op jit(solution)/shard_map/ppermute | solution.py:60
  327.5 27.3 %psum.59 = f32[64,64]{0,1:T(8,128)S(1)} all-reduce(f32[64,64]{0,1:T(8,128)S(1)} %fusion.121), channel_id=1, replica_groups=mesh['blk'=8,'rows'=4] {'blk'}, use_global_device_ids=true, to_apply=%region_5.10 | all-reduce | flops 4096 | bytes 32768 | tf_op jit(solution)/shard_map/psum | solution.py:31
  372.2 10.4 %fusion.60 = f32[64,256,128]{2,0,1:T(8,128)S(1)} fusion(bf16[256,128,128]{2,1,0:T(8,128)(2,1)} %param.12, bf16[256,64,128]{2,1,0:T(8,128)(2,1)} %gather_fusion.4, pred[256]{0:T(512)(128)(4,1)S(1)} %get-tuple-element.8), kind=kOutput, calls=%fused_computation.60 | convolution fusion | flops 538968064 | bytes 20971776 | tf_op jit(solution)/shard_map/kst,sit->ksi/dot_general | solution.py:15
  382.6 7.9 %fusion.6 = f32[8,64,128]{2,0,1:T(8,128)S(1)} fusion(f32[64,256,128]{2,0,1:T(8,128)S(1)} %fusion.60, s32[256]{0:T(256)S(1)} %bitcast.256, pred[256]{0:T(512)(128)(4,1)S(1)} %iota_compare_fusion.4), kind=kOutput, calls=%fused_computation.14 | convolution fusion | flops 201330688 | bytes 8652032 | tf_op jit(solution)/shard_map/ksi,rs->kri/dot_general | solution.py:16
  390.6 25.2 %all-reduce.6 = bf16[64,1024]{1,0:T(8,128)(2,1)S(1)} all-reduce(f32[64,1024]{1,0:T(8,128)S(1)} %bitcast.250), channel_id=1, replica_groups=mesh['blk'=8,'rows'=4] {'blk'}, use_global_device_ids=true, to_apply=%region_6.11 | all-reduce | flops 65536 | bytes 393216 | tf_op jit(solution)/shard_map/psum | solution.py:55
  418.8 7.0 fusion.63
  425.8 7.7 %fusion.4 = f32[32,64,128]{2,0,1:T(8,128)S(1)} fusion(f32[64,256,128]{2,0,1:T(8,128)S(1)} %fusion.63, s32[256]{0:T(256)S(1)} %bitcast.262, pred[256]{0:T(512)(128)(4,1)S(1)} %iota_compare_fusion.4), kind=kOutput, calls=%fused_computation.12 | convolution fusion | flops 805322752 | bytes 9438464 | tf_op jit(solution)/shard_map/ksj,cs->kcj/dot_general | solution.py:25
  435.6 21.7 %collective-permute-done.4 = f32[64,4096]{1,0:T(8,128)S(1)} collective-permute-done((f32[64,4096]{1,0:T(8,128)S(1)}, f32[64,4096]{1,0:T(8,128)S(1)}, u32[]{:S(2)}, u32[]{:S(2)}) %collective-permute-start.4) | collective-permute-done | bytes 1048608 | tf_op jit(solution)/shard_map/ppermute | solution.py:60
  461.0 43.0 %collective-permute-done.5 = f32[64,4096]{1,0:T(8,128)S(1)} collective-permute-done((f32[64,4096]{1,0:T(8,128)S(1)}, f32[64,4096]{1,0:T(8,128)S(1)}, u32[]{:S(2)}, u32[]{:S(2)}) %collective-permute-start.5) | collective-permute-done | bytes 1048608 | tf_op jit(solution)/shard_map/ppermute | solution.py:60
  505.1 26.3 %psum.61 = f32[64,64]{0,1:T(8,128)S(1)} all-reduce(f32[64,64]{0,1:T(8,128)S(1)} %fusion.122), channel_id=1, replica_groups=mesh['blk'=8,'rows'=4] {'blk'}, use_global_device_ids=true, to_apply=%region_7.12 | all-reduce | flops 4096 | bytes 32768 | tf_op jit(solution)/shard_map/psum | solution.py:31
  548.7 10.4 %fusion.66 = f32[64,256,128]{2,0,1:T(8,128)S(1)} fusion(bf16[256,128,128]{2,1,0:T(8,128)(2,1)} %param.12, bf16[256,64,128]{2,1,0:T(8,128)(2,1)} %gather_fusion.6, pred[256]{0:T(512)(128)(4,1)S(1)} %get-tuple-element.8), kind=kOutput, calls=%fused_computation.62 | convolution fusion | flops 538968064 | bytes 20971776 | tf_op jit(solution)/shard_map/kst,sit->ksi/dot_general | solution.py:15
  559.1 7.7 %fusion.2 = f32[8,64,128]{2,0,1:T(8,128)S(1)} fusion(f32[64,256,128]{2,0,1:T(8,128)S(1)} %fusion.66, s32[256]{0:T(256)S(1)} %bitcast.257, pred[256]{0:T(512)(128)(4,1)S(1)} %iota_compare_fusion.4), kind=kOutput, calls=%fused_computation.10 | convolution fusion | flops 201330688 | bytes 8652032 | tf_op jit(solution)/shard_map/ksi,rs->kri/dot_general | solution.py:16
  566.9 25.4 %all-reduce.7 = bf16[64,1024]{1,0:T(8,128)(2,1)S(1)} all-reduce(f32[64,1024]{1,0:T(8,128)S(1)} %bitcast.251), channel_id=1, replica_groups=mesh['blk'=8,'rows'=4] {'blk'}, use_global_device_ids=true, to_apply=%region_8.13 | all-reduce | flops 65536 | bytes 393216 | tf_op jit(solution)/shard_map/psum | solution.py:55
  602.3 7.7 %fusion = f32[32,64,128]{2,0,1:T(8,128)S(1)} fusion(f32[64,256,128]{2,0,1:T(8,128)S(1)} %fusion.69, s32[256]{0:T(256)S(1)} %bitcast.263, pred[256]{0:T(512)(128)(4,1)S(1)} %iota_compare_fusion.4), kind=kOutput, calls=%fused_computation.8 | convolution fusion | flops 805322752 | bytes 9438464 | tf_op jit(solution)/shard_map/ksj,cs->kcj/dot_general | solution.py:25
  612.1 21.1 %collective-permute-done.6 = f32[64,4096]{1,0:T(8,128)S(1)} collective-permute-done((f32[64,4096]{1,0:T(8,128)S(1)}, f32[64,4096]{1,0:T(8,128)S(1)}, u32[]{:S(2)}, u32[]{:S(2)}) %collective-permute-start.6) | collective-permute-done | bytes 1048608 | tf_op jit(solution)/shard_map/ppermute | solution.py:60
  640.3 40.0 %collective-permute-done.7 = f32[64,4096]{1,0:T(8,128)} collective-permute-done((f32[64,4096]{1,0:T(8,128)S(1)}, f32[64,4096]{1,0:T(8,128)}, u32[]{:S(2)}, u32[]{:S(2)}) %collective-permute-start.7) | collective-permute-done | bytes 1048608 | tf_op jit(solution)/shard_map/ppermute | solution.py:60
  682.7 26.7 %psum.63 = f32[64,64]{0,1:T(8,128)S(1)} all-reduce(f32[64,64]{0,1:T(8,128)S(1)} %fusion.123), channel_id=1, replica_groups=mesh['blk'=8,'rows'=4] {'blk'}, use_global_device_ids=true, to_apply=%region_9.14 | all-reduce | flops 4096 | bytes 32768 | tf_op jit(solution)/shard_map/psum | solution.py:31
  (105 shorter events, 122.9 us)
Async XLA Ops:
  0.0 2.8 copy-start
  6.0 10.4 %copy-start.5 = (s32[256,1]{0,1:T(1,128)S(1)}, s32[256,1]{0,1:T(1,128)}, u32[]{:S(2)}) copy-start(s32[256,1]{0,1:T(1,128)} %param.14) | copy-start | bytes 3076
  55.7 7.0 copy-start.6
  71.1 22.4 %collective-permute-start = (f32[64,4096]{1,0:T(8,128)S(1)}, f32[64,4096]{1,0:T(8,128)S(1)}, u32[]{:S(2)}, u32[]{:S(2)}) collective-permute-start(f32[64,4096]{1,0:T(8,128)S(1)} %bitcast.244), channel_id=1, source_target_pairs={{0,1},{1,0},{2,3},{3,2},{4,5},{5,4},{6,7},{7,6},{8,9},{9,8},{10,11... | collective-permute-start | bytes 3145736 | tf_op jit(solution)/shard_map/ppermute | solution.py:60
  103.9 44.9 %collective-permute-start.1 = (f32[64,4096]{1,0:T(8,128)S(1)}, f32[64,4096]{1,0:T(8,128)S(1)}, u32[]{:S(2)}, u32[]{:S(2)}) collective-permute-start(f32[64,4096]{1,0:T(8,128)S(1)} %fusion.116), channel_id=1, source_target_pairs={{0,2},{1,3},{2,0},{3,1},{4,6},{5,7},{6,4},{7,5},{8,10},{9,11},{10,... | collective-permute-start | bytes 3145736 | tf_op jit(solution)/shard_map/ppermute | solution.py:60
  191.0 1.0 copy-start.2
  257.3 22.5 %collective-permute-start.2 = (f32[64,4096]{1,0:T(8,128)S(1)}, f32[64,4096]{1,0:T(8,128)S(1)}, u32[]{:S(2)}, u32[]{:S(2)}) collective-permute-start(f32[64,4096]{1,0:T(8,128)S(1)} %bitcast.245), channel_id=1, source_target_pairs={{0,1},{1,0},{2,3},{3,2},{4,5},{5,4},{6,7},{7,6},{8,9},{9,8},{10,11... | collective-permute-start | bytes 3145736 | tf_op jit(solution)/shard_map/ppermute | solution.py:60
  280.7 45.8 %collective-permute-start.3 = (f32[64,4096]{1,0:T(8,128)S(1)}, f32[64,4096]{1,0:T(8,128)S(1)}, u32[]{:S(2)}, u32[]{:S(2)}) collective-permute-start(f32[64,4096]{1,0:T(8,128)S(1)} %fusion.117), channel_id=1, source_target_pairs={{0,2},{1,3},{2,0},{3,1},{4,6},{5,7},{6,4},{7,5},{8,10},{9,11},{10,... | collective-permute-start | bytes 3145736 | tf_op jit(solution)/shard_map/ppermute | solution.py:60
  368.1 1.0 copy-start.3
  434.2 23.1 %collective-permute-start.4 = (f32[64,4096]{1,0:T(8,128)S(1)}, f32[64,4096]{1,0:T(8,128)S(1)}, u32[]{:S(2)}, u32[]{:S(2)}) collective-permute-start(f32[64,4096]{1,0:T(8,128)S(1)} %bitcast.246), channel_id=1, source_target_pairs={{0,1},{1,0},{2,3},{3,2},{4,5},{5,4},{6,7},{7,6},{8,9},{9,8},{10,11... | collective-permute-start | bytes 3145736 | tf_op jit(solution)/shard_map/ppermute | solution.py:60
  458.1 45.9 %collective-permute-start.5 = (f32[64,4096]{1,0:T(8,128)S(1)}, f32[64,4096]{1,0:T(8,128)S(1)}, u32[]{:S(2)}, u32[]{:S(2)}) collective-permute-start(f32[64,4096]{1,0:T(8,128)S(1)} %fusion.118), channel_id=1, source_target_pairs={{0,2},{1,3},{2,0},{3,1},{4,6},{5,7},{6,4},{7,5},{8,10},{9,11},{10,... | collective-permute-start | bytes 3145736 | tf_op jit(solution)/shard_map/ppermute | solution.py:60
  544.6 1.0 copy-start.4
  610.7 22.6 %collective-permute-start.6 = (f32[64,4096]{1,0:T(8,128)S(1)}, f32[64,4096]{1,0:T(8,128)S(1)}, u32[]{:S(2)}, u32[]{:S(2)}) collective-permute-start(f32[64,4096]{1,0:T(8,128)S(1)} %bitcast.247), channel_id=1, source_target_pairs={{0,1},{1,0},{2,3},{3,2},{4,5},{5,4},{6,7},{7,6},{8,9},{9,8},{10,11... | collective-permute-start | bytes 3145736 | tf_op jit(solution)/shard_map/ppermute | solution.py:60
  634.2 46.2 %collective-permute-start.7 = (f32[64,4096]{1,0:T(8,128)S(1)}, f32[64,4096]{1,0:T(8,128)}, u32[]{:S(2)}, u32[]{:S(2)}) collective-permute-start(f32[64,4096]{1,0:T(8,128)S(1)} %fusion.119), channel_id=1, source_target_pairs={{0,2},{1,3},{2,0},{3,1},{4,6},{5,7},{6,4},{7,5},{8,10},{9,11},{10,... | collective-permute-start | bytes 3145736 | tf_op jit(solution)/shard_map/ppermute | solution.py:60
  680.3 43.4 %copy-start.1 = (bf16[64,4096]{1,0:T(8,128)(2,1)S(1)}, bf16[64,4096]{1,0:T(8,128)(2,1)}, u32[]{:S(2)}) copy-start(bf16[64,4096]{1,0:T(8,128)(2,1)} %param.13) | copy-start | bytes 1572868
